TPU v7x, 256 devices: a whole 4x4x8 slice. The times are simulated.
256 devices in a mesh: dp: 32 (over z, x_hi, core), mp: 8 (over y, x_lo).
Axes of the slice: x: 4 (x_hi: 2, x_lo: 2; x = x_hi * 2 + x_lo), y: 4, z: 8, core: 2. Of those that a mesh axis runs over, the one named last changes fastest.
Arguments:
- activations: bfloat16 [2, 4096, 3968], P(None, 'dp'), may hold values from -6 to 6
- out_grads: bfloat16 [2, 4096, 3968], P(None, 'dp', 'mp'), may hold values from -0.29882812 to 0.29882812
- error_memory: bfloat16 [126976, 3968], P('dp', 'mp'), may hold values from -6 to 6
- q_previous: float32 [3968, 32], P('mp'), may hold values from -6 to 6
Outputs:
- new_error: bfloat16 [126976, 3968], P('dp', 'mp')
- p_basis: float32 [3968, 32], P('dp')
- q_factor: float32 [3968, 32], P('mp')
All inputs are finite; a program needn't handle non-finite values.
Results may differ from a plain program's by a relative error of at most 0.001.
Values sent between devices are 32-bit elements; how exact they have to be, the bound alone decides.
A program may use at most 64 MiB of HBM per device.

v0:
```python
import jax
import jax.numpy as jnp
from jax import lax
from jax.sharding import PartitionSpec as P


def cut_along(x, dim, devices):
    before, after = (x.shape[:dim], x.shape[dim + 1 :])
    return jnp.moveaxis(x.reshape(*before, devices, -1, *after), dim, 0)


def sum_at_owner(x, axis, dim):
    devices = lax.axis_size(axis)
    pieces = lax.all_to_all(cut_along(x, dim, devices), axis, 0, 0, tiled=True)
    return jnp.sum(pieces, axis=0)


def from_everyone(x, axis):
    copies = jnp.broadcast_to(x, (lax.axis_size(axis), *x.shape))
    return lax.all_to_all(copies, axis, split_axis=0, concat_axis=0, tiled=True)


def taken_together(x, axis):
    everything = from_everyone(x, axis)
    return jnp.sum(everything, axis=0)


def laid_out(pieces, dim):
    shape = list(pieces.shape[1:])
    shape[dim] *= pieces.shape[0]
    return jnp.moveaxis(pieces, 0, dim).reshape(shape)


def gathered_copies(x, axis, dim):
    return laid_out(from_everyone(x, axis), dim)


def rows_for(lines, devices):
    spare = -len(lines) % devices
    return jnp.pad(lines, [(0, spare)] + [(0, 0)] * (lines.ndim - 1))


def total_of(x, axes):
    lines = x.reshape(-1)
    padded = rows_for(lines, lax.axis_size(axes))
    whole = gathered_copies(sum_at_owner(padded, axes, 0), axes, 0)
    return lax.slice_in_dim(whole, 0, len(lines)).reshape(x.shape)


def body(activations, out_grads, error_memory, q_previous):
    width = activations.shape[2]
    token_rows = activations.reshape(-1, width)
    grad_rows = out_grads.reshape(-1, out_grads.shape[2])
    highest = lax.Precision.HIGHEST
    projected = jnp.dot(grad_rows, q_previous, precision=highest)
    p_partial = jnp.einsum(
        "td,tr->dr", token_rows, projected, precision=highest, preferred_element_type=jnp.float32
    )
    p_partial = p_partial + jnp.dot(
        error_memory, q_previous, precision=highest, preferred_element_type=jnp.float32
    )
    merged = jnp.einsum(
        "td,tf->df", token_rows, grad_rows, preferred_element_type=jnp.float32
    ) + error_memory.astype(jnp.float32)
    p_share = sum_at_owner(p_partial, "dp", 0)
    p_share = taken_together(p_share, "mp")
    gram_total = taken_together(jnp.dot(p_share.T, p_share, precision=highest), "dp")
    lower_factor = jnp.linalg.cholesky(gram_total)
    share_basis = jax.scipy.linalg.solve_triangular(lower_factor, p_share.T, lower=True).T
    p_basis = gathered_copies(share_basis, "dp", 0)
    q_partial = jnp.einsum("df,dr->fr", merged, p_basis, precision=highest)
    q_factor = total_of(q_partial, "dp") / lax.axis_size("dp")
    approx = jnp.dot(p_basis, q_factor.T, precision=highest)
    new_error = (merged - approx).astype(jnp.bfloat16)
    return (new_error, share_basis, q_factor)


def solution(mesh):
    in_specs = (P(None, "dp", None), P(None, "dp", "mp"), P("dp", "mp"), P("mp", None))
    out_specs = (P("dp", "mp"), P("dp", None), P("mp", None))
    return jax.shard_map(body, mesh=mesh, in_specs=in_specs, out_specs=out_specs, check_vma=False)
```

profile of v0, /device:TPU:1, one launch (start us, length us, event | category | flops | bytes accessed | tf_op | source)
XLA Modules:
  0.0 146.8 jit_solution(9229030997181459290)
XLA Ops:
  0.6 0.0 copy-start
  0.6 1.2 copy.29
  1.9 1.2 fusion.4
  3.1 0.0 copy-done
  3.1 1.0 convolution_bitcast_fusion
  4.1 4.0 %convolution_add_fusion = f32[3968,32]{0,1:T(8,128)S(1)} fusion(f32[3968,32]{0,1:T(8,128)S(1)} %convolution_bitcast_fusion, bf16[3968,496]{0,1:T(8,128)(2,1)} %param.6, f32[496,32]{0,1:T(8,128)} %param.7), kind=kOutput, calls=%fused_computation.2 | convolution fusion | flops 755888128 | bytes 5015552 | tf_op jit(solution)/shard_map/dot_general | solution.py:59
  8.1 1.1 reshape.46
  9.2 0.0 copy-start.1
  9.2 0.3 copy.30
  9.5 29.2 %all_to_all.36 = f32[32,124,32]{1,2,0:T(8,128)S(1)} all-to-all(f32[32,124,32]{1,2,0:T(8,128)S(1)} %copy.30), channel_id=1, replica_groups=mesh['dp'=32,'mp'=8] {'dp'}, dimensions={0} | all-to-all | bytes 1015808 | tf_op jit(solution)/shard_map/all_to_all | solution.py:14
  38.7 0.1 reduce_sum.36
  38.8 9.6 %all_to_all.37 = f32[8,124,32]{1,2,0:T(8,128)S(1)} all-to-all(f32[8,124,32]{1,2,0:T(8,128)S(1)} %broadcast_in_dim.14), channel_id=1, replica_groups=mesh['dp'=32,'mp'=8] {'mp'}, dimensions={0} | all-to-all | bytes 253952 | tf_op jit(solution)/shard_map/all_to_all | solution.py:20
  48.4 0.1 fusion.5
  48.5 0.1 broadcast_in_dim.15
  48.6 0.3 reshape.50
  48.9 18.4 %all_to_all.38 = f32[32,1,1024]{2,1,0:T(1,128)S(1)} all-to-all(f32[32,1,1024]{2,1,0:T(1,128)S(1)} %reshape.50), channel_id=1, replica_groups=mesh['dp'=32,'mp'=8] {'dp'}, dimensions={0} | all-to-all | bytes 262144 | tf_op jit(solution)/shard_map/all_to_all | solution.py:20
  67.3 0.5 broadcast.63
  67.8 1.0 reduce.9
  68.7 0.2 reshape.51
  68.9 0.1 reduce_sum.38
  69.0 0.1 copy.32
  69.0 2.9 %cholesky.16 = f32[32,32]{1,0:T(8,128)S(1)} custom-call(f32[32,32]{1,0:T(8,128)S(1)} %fusion.3), custom_call_target="Cholesky" | custom-call | tf_op jit(solution)/shard_map/jit(cholesky)/cholesky | solution.py:68
  72.0 0.6 compare_reduce_fusion
  72.6 0.7 fusion
  73.3 2.4 %custom-call.7 = f32[1,32,32]{1,2,0:T(8,128)S(1)} custom-call(f32[1,32,32]{2,1,0:T(8,128)S(1)} %fusion), custom_call_target="InvertDiagBlocksLowerTriangular" | custom-call | tf_op jit(solution)/shard_map/jit(_solve_triangular)/triangular_solve | solution.py:69
  75.7 0.2 fusion.1
  76.0 0.0 copy-start.2
  76.0 0.9 broadcast_in_dim.16
  76.8 3.9 %all-to-all-start.3 = ((f32[32,124,32]{1,2,0:T(8,128)}), f32[32,124,32]{1,2,0:T(8,128)S(1)}, u32[]{:S(2)}, u32[]{:S(2)}) async-start(f32[32,124,32]{1,2,0:T(8,128)} %broadcast_in_dim.16), calls=%async_computation.3 | async-start | bytes 1048576 | tf_op jit(solution)/shard_map/all_to_all | solution.py:20
  80.7 0.0 copy-done.1
  80.7 6.4 %bitcast_add_fusion = f32[3968,496]{0,1:T(8,128)} fusion(bf16[3968,496]{0,1:T(8,128)(2,1)} %param.6, bf16[2,128,496]{1,2,0:T(8,128)(2,1)S(1)} %copy-done.1, bf16[2,128,3968]{2,1,0:T(8,128)(2,1)S(1)} %copy-done), kind=kOutput, calls=%fused_computation | convolution fusion | flops 1011617792 | bytes 14094336 | tf_op jit(solution)/shard_map/td,tf->df/dot_general | solution.py:62
  87.1 0.0 copy-done.2
  87.1 10.8 %all-to-all-done.3 = f32[32,124,32]{1,2,0:T(8,128)S(1)} async-done(((f32[32,124,32]{1,2,0:T(8,128)}), f32[32,124,32]{1,2,0:T(8,128)S(1)}, u32[]{:S(2)}, u32[]{:S(2)}) %all-to-all-start.3) | async-done | bytes 507936 | tf_op jit(solution)/shard_map/all_to_all | solution.py:20
  97.9 0.3 copy.33
  98.2 0.3 reshape.47
  98.5 8.7 %fusion.6 = f32[496,32]{1,0:T(8,128)S(1)} fusion(f32[3968,496]{0,1:T(8,128)} %bitcast_add_fusion, f32[3968,32]{0,1:T(8,128)S(1)} %reshape.47), kind=kOutput, calls=%fused_computation.17 | convolution fusion | flops 755761152 | bytes 8443904 | tf_op jit(solution)/shard_map/df,dr->fr/dot_general | solution.py:71
  107.3 0.2 all_to_all.29
  107.5 15.1 %all_to_all.39 = f32[32,1,496]{2,1,0:T(1,128)S(1)} all-to-all(f32[32,1,496]{2,1,0:T(1,128)S(1)} %all_to_all.29), channel_id=1, replica_groups=mesh['dp'=32,'mp'=8] {'dp'}, dimensions={0} | all-to-all | bytes 126976 | tf_op jit(solution)/shard_map/all_to_all | solution.py:14
  122.5 0.1 reduce_sum.39
  122.6 12.9 %all_to_all.40 = f32[32,1,496]{2,1,0:T(1,128)S(1)} all-to-all(f32[32,1,496]{2,1,0:T(1,128)S(1)} %broadcast_in_dim.17), channel_id=1, replica_groups=mesh['dp'=32,'mp'=8] {'dp'}, dimensions={0} | all-to-all | bytes 126976 | tf_op jit(solution)/shard_map/all_to_all | solution.py:20
  135.5 0.2 multiply_reduce_fusion
  135.7 0.1 div.20
  135.9 10.2 %subtract_convert_fusion = bf16[3968,496]{0,1:T(8,128)(2,1)} fusion(f32[3968,496]{0,1:T(8,128)} %bitcast_add_fusion, f32[3968,32]{0,1:T(8,128)S(1)} %reshape.47, f32[496,32]{1,0:T(8,128)S(1)} %div.20), kind=kOutput, calls=%fused_computation.1 | convolution fusion | flops 759697408 | bytes 12380160 | tf_op jit(solution)/shard_map/dot_general | solution.py:73
  146.1 0.7 copy.36
  (5 shorter events, 0.1 us)
Async XLA Ops:
  0.6 2.4 %copy-start = (bf16[2,128,3968]{2,1,0:T(8,128)(2,1)S(1)}, bf16[2,128,3968]{2,1,0:T(8,128)(2,1)}, u32[]{:S(2)}) copy-start(bf16[2,128,3968]{2,1,0:T(8,128)(2,1)} %param.4) | copy-start | bytes 6094852
  9.2 71.5 %copy-start.1 = (bf16[2,128,496]{1,2,0:T(8,128)(2,1)S(1)}, bf16[2,128,496]{1,2,0:T(8,128)(2,1)}, u32[]{:S(2)}) copy-start(bf16[2,128,496]{1,2,0:T(8,128)(2,1)} %param.5) | copy-start | bytes 761860
  76.0 11.2 %copy-start.2 = (f32[124,32]{0,1:T(8,128)}, f32[124,32]{0,1:T(8,128)S(1)}, u32[]{:S(2)}) copy-start(f32[124,32]{0,1:T(8,128)S(1)} %fusion.1) | copy-start | bytes 47620
  76.8 21.1 %all-to-all-start.3 = ((f32[32,124,32]{1,2,0:T(8,128)}), f32[32,124,32]{1,2,0:T(8,128)S(1)}, u32[]{:S(2)}, u32[]{:S(2)}) async-start(f32[32,124,32]{1,2,0:T(8,128)} %broadcast_in_dim.16), calls=%async_computation.3 | async-start | bytes 1048576 | tf_op jit(solution)/shard_map/all_to_all | solution.py:20
where the time goes:
time: 147 us
  blocking collectives  85.1 us (58%)
  matrix products  31.9 us (22%)
  waiting for transfers between devices  10.8 us (7%)
  other arithmetic  8.02 us (5%)
  local copies, waits for them, and re-layouts  6.3 us (4%)
  starting transfers between devices  3.86 us (3%)
    all_to_all x2, blocking collectives, sum_at_owner(): pieces = lax.all_to_all(cut_along(x, dim, devices), axis, 0, 0, tiled=True)  44.3 us
    all_to_all x3, blocking collectives, from_everyone(): return lax.all_to_all(copies, axis, split_axis=0, concat_axis=0, tiled=True)  40.9 us
    all_to_all x1, waiting for transfers between devices, from_everyone(): return lax.all_to_all(copies, axis, split_axis=0, concat_axis=0, tiled=True)  10.8 us
    dot_general x1, matrix products, body(): approx = jnp.dot(p_basis, q_factor.T, precision=highest)  10.2 us
    dot_general x1, matrix products, body(): q_partial = jnp.einsum('df,dr->fr', merged, p_basis, precision=highest)  8.71 us
    dot_general x1, matrix products, body(): jnp.einsum('td,tf->df', token_rows, grad_rows, preferred_element_type=jnp...  6.42 us
    dot_general x1, matrix products, body(): jnp.dot(error_memory, q_previous, precision=highest, preferred_element_ty...  3.98 us
    all_to_all x1, starting transfers between devices, from_everyone(): return lax.all_to_all(copies, axis, split_axis=0, concat_axis=0, tiled=True)  3.86 us
  transfers between devices with their start and end apart: 1, of which 1 were waited for; matrix products, arithmetic and copies ran while one was open for 4% of the time, Pallas kernels for 0%

commit v1 on v0

v1 whole, which is shorter than its diff:
```python
import functools

import jax
import jax.numpy as jnp
from jax import lax
from jax.experimental import pallas as pl
from jax.experimental.pallas import tpu as pltpu
from jax.sharding import PartitionSpec as P

MESH = pl.DeviceIdType.MESH
F32 = jnp.float32
BF16 = jnp.bfloat16
BLOCKS = 16
LANES = 256


def split3(x):
    high = x.astype(BF16)
    rest = x - high.astype(F32)
    middle = rest.astype(BF16)
    low = (rest - middle.astype(F32)).astype(BF16)
    return jnp.concatenate([high, middle, low], axis=0)


def fold3(x):
    rows = x.shape[0] // 3
    return x[:rows] + x[rows : 2 * rows] + x[2 * rows :]


def dot_nn(a, b):
    return lax.dot_general(a, b, (((1,), (0,)), ((), ())), preferred_element_type=F32)


def dot_nt(a, b, precision=None):
    return lax.dot_general(
        a, b, (((1,), (1,)), ((), ())), preferred_element_type=F32, precision=precision
    )


def inverse_factor(gram):
    n = gram.shape[0]
    rows = lax.broadcasted_iota(jnp.int32, (n, 2 * n), 0)
    columns = lax.broadcasted_iota(jnp.int32, (n, 2 * n), 1)
    identity = jnp.where(rows + n == columns, 1.0, 0.0).astype(F32)
    wide = jnp.where(columns < n, jnp.concatenate([gram, gram], axis=1), identity)
    row_index = lax.broadcasted_iota(jnp.int32, (n, 1), 0)
    for j in range(n):
        pivot = wide[j : j + 1, j : j + 1]
        scale = lax.rsqrt(pivot)
        scale = scale * (1.5 - 0.5 * pivot * scale * scale)
        row = wide[j : j + 1, :] * scale
        factor = wide[:, j : j + 1] * scale
        below = wide - factor * row
        wide = jnp.where(row_index > j, below, jnp.where(row_index == j, row, wide))
    return wide[:, n:]


def reduce_kernel(
    q_hbm, g_hbm, a_hbm, e_hbm,
    merged_ref, basis3_ref, q3_ref, qt_ref, pb_ref,
    qv, gv, av, ev,
    p_part, c_recv, x_src, x_recv, z_buf, p_full, ps,
    w_src, w_recv, w_z, w_full, basis_f,
    load_sem, ssem, rsem,
):
    rank = qv.shape[0]
    half = rank // 2
    width = e_hbm.shape[1]
    share = pb_ref.shape[1]
    dp, mp = lax.axis_index("dp"), lax.axis_index("mp")
    mz, mxh, mc = dp // 4, (dp // 2) % 2, dp % 2
    my, mxl = mp // 2, mp % 2
    mx = mxh * 2 + mxl
    me = my * 4 + mx

    def device(x, y, z, c):
        return ((z * 2 + x // 2) * 2 + c, y * 2 + x % 2)

    def plane_peer(j):
        return (mx + j % 4) % 4, (my + j // 4) % 4

    def group_peer(j):
        return (mxh + j // 2) % 2, (mc + j % 2) % 2

    partner = device(mx, my, mz, (mc + 1) % 2)

    tokens = a_hbm.shape[1]
    loads = [pltpu.make_async_copy(q_hbm, qv, load_sem.at[0])]
    loads[0].start()
    g_loads = []
    for m in range(2):
        cp = pltpu.make_async_copy(g_hbm.at[m], gv.at[:, pl.ds(m * tokens, tokens)], load_sem.at[1 + m])
        cp.start()
        g_loads.append(cp)
    step = 1024
    pieces = [(s, min(step, width - s)) for s in range(0, width, step)]
    piece_loads = []
    for i, (s, n) in enumerate(pieces):
        own = []
        for m in range(2):
            own.append(
                pltpu.make_async_copy(
                    a_hbm.at[m, :, pl.ds(s, n)], av.at[pl.ds(m * tokens, tokens), pl.ds(s, n)], load_sem.at[3 + 3 * i + m]
                )
            )
        own.append(
            pltpu.make_async_copy(e_hbm.at[:, pl.ds(s, n)], ev.at[:, pl.ds(s, n)], load_sem.at[5 + 3 * i])
        )
        for cp in own:
            cp.start()
        piece_loads.append(own)

    barrier = pltpu.get_barrier_semaphore()

    def greet(target):
        pl.semaphore_signal(barrier, inc=1, device_id=target, device_id_type=MESH)

    greet(partner)

    def greet_plane(j, carry):
        x, y = plane_peer(j)
        greet(device(x, y, mz, mc))
        return carry

    lax.fori_loop(1, 16, greet_plane, 0)

    def greet_z(j, carry):
        greet(device(mx, my, (mz + j) % 8, mc))
        return carry

    lax.fori_loop(1, 8, greet_z, 0)
    greet(device(((mxh + 1) % 2) * 2 + mxl, my, mz, (mc + 1) % 2))

    padded = ev.shape[1]
    ev[:, width:] = jnp.zeros((ev.shape[0], padded - width), BF16)
    av[:, width:] = jnp.zeros((av.shape[0], padded - width), BF16)

    loads[0].wait()
    qs = split3(qv[...])
    for cp in g_loads:
        cp.wait()
    gqs = split3(fold3(dot_nn(qs, gv[...])))
    for i, (s, n) in enumerate(pieces):
        for cp in piece_loads[i]:
            cp.wait()
        n = min(step, padded - s)
        r = fold3(dot_nn(qs, ev[:, s : s + n]) + dot_nn(gqs, av[:, s : s + n]))
        for b in range(n // LANES):
            p_part[s // LANES + b] = r[:, b * LANES : (b + 1) * LANES]

    pl.semaphore_wait(barrier, 24)

    def remote(src, dst, phase, target):
        return pltpu.make_async_remote_copy(
            src_ref=src, dst_ref=dst, send_sem=ssem.at[phase], recv_sem=rsem.at[phase],
            device_id=target, device_id_type=MESH,
        )

    mine = pl.ds(pl.multiple_of(mc * half, half), half)
    other = pl.ds(pl.multiple_of(((mc + 1) % 2) * half, half), half)

    swap = remote(p_part.at[:, other, :], c_recv, 0, partner)
    swap.start()
    swap.wait_recv()
    x_src[...] = p_part[:, mine, :] + c_recv[...]

    def send_plane(j, carry):
        x, y = plane_peer(j)
        remote(x_src.at[y * 4 + x], x_recv.at[j], 1, device(x, y, mz, mc)).start()
        return carry

    lax.fori_loop(1, 16, send_plane, 0)
    plane_all = remote(x_src.at[pl.ds(1, 15)], x_recv.at[pl.ds(1, 15)], 1, partner)

    for s in range(0, width, 512):
        n = min(512, width - s)
        merged_ref[:, s : s + n] = dot_nn(gv[...], av[:, s : s + n]) + ev[:, s : s + n].astype(F32)

    plane_all.wait_recv()
    total = x_src[me]
    for j in range(1, 16):
        total = total + x_recv[j]
    z_buf[mz] = total

    def send_z(j, carry):
        remote(z_buf.at[mz], z_buf.at[mz], 2, device(mx, my, (mz + j) % 8, mc)).start()
        return carry

    lax.fori_loop(1, 8, send_z, 0)
    z_all = remote(z_buf.at[pl.ds(0, 7)], z_buf.at[pl.ds(0, 7)], 2, partner)
    z_all.wait_recv()
    total = z_buf[0]
    for j in range(1, 8):
        total = total + z_buf[j]
    p_full[me, mine, :] = total

    def send_gather(j, carry):
        x, y = plane_peer(j)
        remote(p_full.at[me, mine, :], p_full.at[me, mine, :], 3, device(x, y, mz, mc)).start()
        return carry

    lax.fori_loop(1, 16, send_gather, 0)
    gather_all = remote(x_recv.at[pl.ds(1, 15)], x_recv.at[pl.ds(1, 15)], 3, partner)
    gather_all.wait_recv()
    pair = remote(p_full.at[:, mine, :], p_full.at[:, mine, :], 4, partner)
    pair.start()
    pair.wait_recv()

    for b in range(BLOCKS):
        ps[:, b * LANES : (b + 1) * LANES] = split3(p_full[b])
    pas = split3(fold3(dot_nt(ps[...], av[...])))
    wt = fold3(dot_nt(ps[...], ev[...]) + dot_nt(pas, gv[...]))
    for g in range(4):
        w_src[g] = wt[8 * g : 8 * g + 8, :]

    group = mxh * 2 + mc

    def send_group(j, carry):
        xh, c = group_peer(j)
        remote(w_src.at[xh * 2 + c], w_recv.at[j], 5, device(xh * 2 + mxl, my, mz, c)).start()
        return carry

    lax.fori_loop(1, 4, send_group, 0)
    group_all = remote(w_src.at[pl.ds(1, 3)], w_recv.at[pl.ds(1, 3)], 5, partner)

    p_rows = jnp.concatenate([p_full[b] for b in range(BLOCKS)], axis=1)
    basis_f[...] = p_rows
    gram = dot_nt(p_rows, p_rows, lax.Precision.HIGHEST)

    group_all.wait_recv()
    w_z[mz] = w_src[group] + w_recv[1] + w_recv[2] + w_recv[3]

    def send_wz(j, carry):
        remote(w_z.at[mz], w_z.at[mz], 6, device(mx, my, (mz + j) % 8, mc)).start()
        return carry

    lax.fori_loop(1, 8, send_wz, 0)
    wz_all = remote(w_z.at[pl.ds(0, 7)], w_z.at[pl.ds(0, 7)], 6, partner)

    inverse = inverse_factor(gram)

    wz_all.wait_recv()
    total = w_z[0]
    for j in range(1, 8):
        total = total + w_z[j]
    w_full[group] = total

    def send_wg(j, carry):
        xh, c = group_peer(j)
        remote(w_full.at[group], w_full.at[group], 7, device(xh * 2 + mxl, my, mz, c)).start()
        return carry

    lax.fori_loop(1, 4, send_wg, 0)
    wg_all = remote(w_recv.at[pl.ds(1, 3)], w_recv.at[pl.ds(1, 3)], 7, partner)

    basis = jnp.dot(inverse, basis_f[...], precision=lax.Precision.HIGHEST, preferred_element_type=F32)
    basis_f[...] = basis
    high = basis[:, :width].astype(BF16)
    low = (basis[:, :width] - high.astype(F32)).astype(BF16)
    basis3_ref[...] = jnp.concatenate([high, low, high], axis=0)
    start = dp * share
    base = pl.multiple_of((start // 128) * 128, 128)
    window = basis_f[:, pl.ds(base, 256)]
    pb_ref[...] = pltpu.roll(window, (256 - start % 128) % 256, 1)[:, :share]

    wg_all.wait_recv()
    w_rows = jnp.concatenate([w_full[g] for g in range(4)], axis=0)
    qt = jnp.dot(inverse, w_rows, precision=lax.Precision.HIGHEST, preferred_element_type=F32) * (1.0 / 32)
    qt_ref[...] = qt
    q = qt.T
    q_high = q.astype(BF16)
    q_low = (q - q_high.astype(F32)).astype(BF16)
    q3_ref[...] = jnp.concatenate([q_high, q_high, q_low], axis=1)

    swap.wait_send()
    plane_all.wait_send()
    z_all.wait_send()
    gather_all.wait_send()
    pair.wait_send()
    group_all.wait_send()
    wz_all.wait_send()
    wg_all.wait_send()


def error_kernel(merged_ref, basis3_ref, q3_ref, qt_ref, pb_ref, out_hbm, qt_out, pb_out, stage, sem):
    rows, width = merged_ref.shape
    cuts = [(s, min(64, rows - s)) for s in range(0, rows, 64)]
    copies = []
    for i, (s, n) in enumerate(cuts):
        block = merged_ref[s : s + n, :] - dot_nn(q3_ref[s : s + n, :], basis3_ref[...])
        stage[s : s + n, :] = block.astype(BF16)
        cp = pltpu.make_async_copy(stage.at[pl.ds(s, n)], out_hbm.at[pl.ds(s, n)], sem.at[i])
        cp.start()
        copies.append(cp)
    qt_out[...] = qt_ref[...]
    pb_out[...] = pb_ref[...]
    for cp in copies:
        cp.wait()


def body(activations, out_grads, error_memory, q_previous):
    q_t = q_previous.T
    g_t = out_grads.transpose(0, 2, 1)
    e_t = error_memory.T
    rank, columns = q_t.shape
    width = e_t.shape[0 + 1]
    tokens = activations.shape[1]
    share = width // lax.axis_size("dp")
    padded = BLOCKS * LANES
    half = rank // 2
    any_spec = pl.BlockSpec(memory_space=pl.ANY)
    vmem = pl.BlockSpec(memory_space=pltpu.VMEM)
    merged, basis3, q3, qt, pb = pl.pallas_call(
        reduce_kernel,
        out_shape=(
            jax.ShapeDtypeStruct((columns, width), F32),
            jax.ShapeDtypeStruct((3 * rank, width), BF16),
            jax.ShapeDtypeStruct((columns, 3 * rank), BF16),
            jax.ShapeDtypeStruct((rank, columns), F32),
            jax.ShapeDtypeStruct((rank, share), F32),
        ),
        in_specs=[pl.BlockSpec(memory_space=pltpu.HBM)] * 4,
        out_specs=(vmem,) * 5,
        scratch_shapes=[
            pltpu.VMEM((rank, columns), F32),
            pltpu.VMEM((columns, 2 * tokens), BF16),
            pltpu.VMEM((2 * tokens, padded), BF16),
            pltpu.VMEM((columns, padded), BF16),
            pltpu.VMEM((BLOCKS, rank, LANES), F32),
            pltpu.VMEM((BLOCKS, half, LANES), F32),
            pltpu.VMEM((BLOCKS, half, LANES), F32),
            pltpu.VMEM((BLOCKS, half, LANES), F32),
            pltpu.VMEM((8, half, LANES), F32),
            pltpu.VMEM((BLOCKS, rank, LANES), F32),
            pltpu.VMEM((3 * rank, padded), BF16),
            pltpu.VMEM((4, 8, columns), F32),
            pltpu.VMEM((4, 8, columns), F32),
            pltpu.VMEM((8, 8, columns), F32),
            pltpu.VMEM((4, 8, columns), F32),
            pltpu.VMEM((rank, padded), F32),
            pltpu.SemaphoreType.DMA((16,)),
            pltpu.SemaphoreType.DMA((8,)),
            pltpu.SemaphoreType.DMA((8,)),
        ],
        compiler_params=pltpu.CompilerParams(
            collective_id=0, has_side_effects=True, vmem_limit_bytes=28 << 20
        ),
        name="reduce_kernel",
    )(*[pltpu.with_memory_space_constraint(x, pltpu.HBM) for x in (q_t, g_t, activations, e_t)])
    new_t, q_out, pb_out = pl.pallas_call(
        error_kernel,
        out_shape=(
            jax.ShapeDtypeStruct((columns, width), BF16),
            jax.ShapeDtypeStruct((rank, columns), F32),
            jax.ShapeDtypeStruct((rank, share), F32),
        ),
        in_specs=[vmem] * 5,
        out_specs=(any_spec, vmem, vmem),
        scratch_shapes=[pltpu.VMEM((columns, width), BF16), pltpu.SemaphoreType.DMA((8,))],
        compiler_params=pltpu.CompilerParams(vmem_limit_bytes=20 << 20),
        name="error_kernel",
    )(merged, basis3, q3, qt, pb)
    return new_t.T, pb_out.T, q_out.T


def solution(mesh):
    in_specs = (P(None, "dp", None), P(None, "dp", "mp"), P("dp", "mp"), P("mp", None))
    out_specs = (P("dp", "mp"), P("dp", None), P("mp", None))
    return jax.shard_map(body, mesh=mesh, in_specs=in_specs, out_specs=out_specs, check_vma=False)
```

time: 147 us -> 51.8 us (0.35)
  blocking collectives: 85.1 us -> 0 us
  Pallas kernels: 0 us -> 51 us
  matrix products: 31.9 us -> 0 us
  waiting for transfers between devices: 10.8 us -> 0 us
  other arithmetic: 8.02 us -> 0 us
  local copies, waits for them, and re-layouts: 6.3 us -> 0 us
  starting transfers between devices: 3.86 us -> 0 us
    all_to_all x5 -> x0, blocking collectives: 85.1 us -> none  [the longest x2 44.3 us: sum_at_owner(): pieces = lax.all_to_all(cut_along(x, dim, devices), axis, 0, 0, tiled=True)]
    pallas_call x0 -> x2, Pallas kernels: none -> 51 us  [the longest x1 48.1 us: body(): pl.pallas_call(reduce_kernel, out_shape=(jax.ShapeDtypeStruct((columns, w...]
    dot_general x7 -> x0, matrix products: 31.7 us -> none  [the longest x1 10.2 us: body(): approx = jnp.dot(p_basis, q_factor.T, precision=highest)]
    all_to_all x1 -> x0, waiting for transfers between devices: 10.8 us -> none  [from_everyone(): return lax.all_to_all(copies, axis, split_axis=0, concat_axis=0, tiled=True)]
    another operation x5 -> x0, other arithmetic: 6.68 us -> none  [the longest x3 3.6 us: body(): lower_factor = jnp.linalg.cholesky(gram_total)]
    all_to_all x1 -> x0, starting transfers between devices: 3.86 us -> none  [from_everyone(): return lax.all_to_all(copies, axis, split_axis=0, concat_axis=0, tiled=True)]
    unnamed x10 -> x0, local copies, waits for them, and re-layouts: 2.41 us -> none
    reshape x3 -> x0, local copies, waits for them, and re-layouts: 1.72 us -> none  [the longest x2 1.38 us: cut_along(): return jnp.moveaxis(x.reshape(*before, devices, -1, *after), dim, 0)]
  transfers between devices with their start and end apart: 1 -> 0, of which waited for: 1 -> 0; matrix products, arithmetic and copies ran while one was open for 4% -> 0% of each run, Pallas kernels for 0% -> 0%
where the time goes in v1:
time: 51.8 us; the launch traced here: 51.7 us
  Pallas kernels  51 us (98%)
  between operations  0.64 us (1%)
    pallas_call x1, Pallas kernels, body(): pl.pallas_call(reduce_kernel, out_shape=(jax.ShapeDtypeStruct((columns, w...  48.1 us
    pallas_call x1, Pallas kernels, body(): pl.pallas_call(error_kernel, out_shape=(jax.ShapeDtypeStruct((columns, wi...  2.9 us

profile of v1, /device:TPU:1, one launch (start us, length us, event | category | flops | bytes accessed | tf_op | source)
XLA Modules:
  0.0 51.7 jit_solution(13817615491158783887)
XLA Ops:
  0.6 48.1 %reduce_kernel.1 = (f32[496,3968]{1,0:T(8,128)S(1)}, bf16[96,3968]{1,0:T(8,128)(2,1)S(1)}, bf16[496,96]{1,0:T(8,128)(2,1)S(1)}, f32[32,496]{1,0:T(8,128)S(1)}, f32[32,124]{1,0:T(8,128)S(1)}) custom-call(f32[32,496]{1,0:T(8,128)} %bitcast.8, bf16[2,496,128]{2,1,0:T(8,128)(2,1)} %bitcast.7, bf16[2,128,3968]{2,1,0:T(8,128)(2,1)} %a_hbm.1, bf16[496,3968]{1,0:T(8,128)(2,1)} %bitcast.6), custom_call_target="tpu_custom_call" | custom-call | tf_op jit(solution)/shard_map/reduce_kernel/pallas_call | solution.py:313
  48.8 2.9 %error_kernel.1 = (bf16[496,3968]{1,0:T(8,128)(2,1)}, f32[32,496]{1,0:T(8,128)}, f32[32,124]{1,0:T(8,128)}) custom-call(f32[496,3968]{1,0:T(8,128)S(1)} %get-tuple-element.11.merged_ref, bf16[96,3968]{1,0:T(8,128)(2,1)S(1)} %get-tuple-element.12.basis3_ref, bf16[496,96]{1,0:T(8,128)(2,1)S(1)} %get-tuple-element.13.q3_ref, ...), custom_call_target="tpu_custom_call" | custom-call | tf_op jit(solution)/shard_map/error_kernel/pallas_call | solution.py:350

commit v2 on v1

--- a/solution.py
+++ b/solution.py
@@ -12,6 +12,14 @@
 BF16 = jnp.bfloat16
 BLOCKS = 16
 LANES = 256
+ROW_ORDER = (2, 3, 1, 0)
+X_ORDER = (2, 3, 1, 0)
+Z_ORDER = (4, 3, 5, 2, 6, 1, 7)
+PLANE_FAR_FIRST = sorted(
+    ((dx, dy) for dx in range(4) for dy in range(4) if dx + dy),
+    key=lambda d: -(min(d[0], 4 - d[0]) + min(d[1], 4 - d[1])),
+)
+LAG = 3
 
 
 def split3(x):
@@ -59,7 +67,7 @@
     q_hbm, g_hbm, a_hbm, e_hbm,
     merged_ref, basis3_ref, q3_ref, qt_ref, pb_ref,
     qv, gv, av, ev,
-    p_part, c_recv, x_src, x_recv, z_buf, p_full, ps,
+    p_part, c_recv, x_src, x_recv, z_buf, p_full, acc,
     w_src, w_recv, w_z, w_full, basis_f,
     load_sem, ssem, rsem,
 ):
@@ -85,6 +93,7 @@
     partner = device(mx, my, mz, (mc + 1) % 2)
 
     tokens = a_hbm.shape[1]
+    padded = ev.shape[1]
     loads = [pltpu.make_async_copy(q_hbm, qv, load_sem.at[0])]
     loads[0].start()
     g_loads = []
@@ -92,23 +101,37 @@
         cp = pltpu.make_async_copy(g_hbm.at[m], gv.at[:, pl.ds(m * tokens, tokens)], load_sem.at[1 + m])
         cp.start()
         g_loads.append(cp)
-    step = 1024
-    pieces = [(s, min(step, width - s)) for s in range(0, width, step)]
-    piece_loads = []
-    for i, (s, n) in enumerate(pieces):
-        own = []
-        for m in range(2):
-            own.append(
+    step = padded // 4
+    short = width - 3 * step
+    pieces = []
+    for i, dy in enumerate(ROW_ORDER):
+        row = (my + dy) % 4
+        start = pl.multiple_of(row * step, step)
+
+        def piece_copies(n, start=start, i=i):
+            lanes = pl.ds(start, n)
+            copies = [
                 pltpu.make_async_copy(
-                    a_hbm.at[m, :, pl.ds(s, n)], av.at[pl.ds(m * tokens, tokens), pl.ds(s, n)], load_sem.at[3 + 3 * i + m]
+                    a_hbm.at[m, :, lanes], av.at[pl.ds(m * tokens, tokens), lanes], load_sem.at[3 + 3 * i + m]
                 )
-            )
-        own.append(
-            pltpu.make_async_copy(e_hbm.at[:, pl.ds(s, n)], ev.at[:, pl.ds(s, n)], load_sem.at[5 + 3 * i])
-        )
-        for cp in own:
-            cp.start()
-        piece_loads.append(own)
+                for m in range(2)
+            ]
+            copies.append(pltpu.make_async_copy(e_hbm.at[:, lanes], ev.at[:, lanes], load_sem.at[5 + 3 * i]))
+            return copies
+
+        def each(action, row=row, piece_copies=piece_copies):
+            @pl.when(row < 3)
+            def _():
+                for cp in piece_copies(step):
+                    action(cp)
+
+            @pl.when(row == 3)
+            def _():
+                for cp in piece_copies(short):
+                    action(cp)
+
+        each(lambda cp: cp.start())
+        pieces.append((dy, row, start, each))
 
     barrier = pltpu.get_barrier_semaphore()
 
@@ -131,7 +154,6 @@
     lax.fori_loop(1, 8, greet_z, 0)
     greet(device(((mxh + 1) % 2) * 2 + mxl, my, mz, (mc + 1) % 2))
 
-    padded = ev.shape[1]
     ev[:, width:] = jnp.zeros((ev.shape[0], padded - width), BF16)
     av[:, width:] = jnp.zeros((av.shape[0], padded - width), BF16)
 
@@ -140,37 +162,42 @@
     for cp in g_loads:
         cp.wait()
     gqs = split3(fold3(dot_nn(qs, gv[...])))
-    for i, (s, n) in enumerate(pieces):
-        for cp in piece_loads[i]:
-            cp.wait()
-        n = min(step, padded - s)
-        r = fold3(dot_nn(qs, ev[:, s : s + n]) + dot_nn(gqs, av[:, s : s + n]))
-        for b in range(n // LANES):
-            p_part[s // LANES + b] = r[:, b * LANES : (b + 1) * LANES]
-
-    pl.semaphore_wait(barrier, 24)
-
-    def remote(src, dst, phase, target):
+
+    def remote(src, dst, send, recv, target):
         return pltpu.make_async_remote_copy(
-            src_ref=src, dst_ref=dst, send_sem=ssem.at[phase], recv_sem=rsem.at[phase],
+            src_ref=src, dst_ref=dst, send_sem=ssem.at[send], recv_sem=rsem.at[recv],
             device_id=target, device_id_type=MESH,
         )
 
     mine = pl.ds(pl.multiple_of(mc * half, half), half)
     other = pl.ds(pl.multiple_of(((mc + 1) % 2) * half, half), half)
-
-    swap = remote(p_part.at[:, other, :], c_recv, 0, partner)
-    swap.start()
-    swap.wait_recv()
-    x_src[...] = p_part[:, mine, :] + c_recv[...]
-
-    def send_plane(j, carry):
-        x, y = plane_peer(j)
-        remote(x_src.at[y * 4 + x], x_recv.at[j], 1, device(x, y, mz, mc)).start()
-        return carry
-
-    lax.fori_loop(1, 16, send_plane, 0)
-    plane_all = remote(x_src.at[pl.ds(1, 15)], x_recv.at[pl.ds(1, 15)], 1, partner)
+    swaps = []
+
+    def to_plane(i):
+        dy, row, _, _ = pieces[i]
+        four = pl.ds(row * 4, 4)
+        swaps[i].wait_recv()
+        x_src[four] = p_part[four, mine, :] + c_recv[four]
+        for dx in X_ORDER:
+            if dx + dy > 0:
+                x = (mx + dx) % 4
+                remote(x_src.at[row * 4 + x], x_recv.at[dy * 4 + dx], 1, 1, device(x, row, mz, mc)).start()
+
+    for i, (dy, row, start, each) in enumerate(pieces):
+        each(lambda cp: cp.wait())
+        lanes = pl.ds(start, step)
+        r = fold3(dot_nn(qs, ev[:, lanes]) + dot_nn(gqs, av[:, lanes]))
+        for b in range(4):
+            p_part[row * 4 + b] = r[:, b * LANES : (b + 1) * LANES]
+        if i == 0:
+            pl.semaphore_wait(barrier, 24)
+        four = pl.ds(row * 4, 4)
+        swaps.append(remote(p_part.at[four, other, :], c_recv.at[four], 8 + i, 8 + i, partner))
+        swaps[i].start()
+        if i > 0:
+            to_plane(i - 1)
+    to_plane(3)
+    plane_all = remote(x_src.at[pl.ds(1, 15)], x_recv.at[pl.ds(1, 15)], 1, 1, partner)
 
     for s in range(0, width, 512):
         n = min(512, width - s)
@@ -182,46 +209,56 @@
         total = total + x_recv[j]
     z_buf[mz] = total
 
-    def send_z(j, carry):
-        remote(z_buf.at[mz], z_buf.at[mz], 2, device(mx, my, (mz + j) % 8, mc)).start()
-        return carry
-
-    lax.fori_loop(1, 8, send_z, 0)
-    z_all = remote(z_buf.at[pl.ds(0, 7)], z_buf.at[pl.ds(0, 7)], 2, partner)
+    for dz in Z_ORDER:
+        remote(z_buf.at[mz], z_buf.at[mz], 2, 2, device(mx, my, (mz + dz) % 8, mc)).start()
+    z_all = remote(z_buf.at[pl.ds(0, 7)], z_buf.at[pl.ds(0, 7)], 2, 2, partner)
+    acc[...] = jnp.zeros_like(acc)
     z_all.wait_recv()
     total = z_buf[0]
     for j in range(1, 8):
         total = total + z_buf[j]
     p_full[me, mine, :] = total
 
-    def send_gather(j, carry):
-        x, y = plane_peer(j)
-        remote(p_full.at[me, mine, :], p_full.at[me, mine, :], 3, device(x, y, mz, mc)).start()
-        return carry
-
-    lax.fori_loop(1, 16, send_gather, 0)
-    gather_all = remote(x_recv.at[pl.ds(1, 15)], x_recv.at[pl.ds(1, 15)], 3, partner)
-    gather_all.wait_recv()
-    pair = remote(p_full.at[:, mine, :], p_full.at[:, mine, :], 4, partner)
-    pair.start()
-    pair.wait_recv()
-
-    for b in range(BLOCKS):
-        ps[:, b * LANES : (b + 1) * LANES] = split3(p_full[b])
-    pas = split3(fold3(dot_nt(ps[...], av[...])))
-    wt = fold3(dot_nt(ps[...], ev[...]) + dot_nt(pas, gv[...]))
+    def block_copy(k, recv, target):
+        return remote(p_full.at[k, mine, :], p_full.at[k, mine, :], 3 if recv < 32 else 4, recv, target)
+
+    for dx, dy in PLANE_FAR_FIRST:
+        block_copy(me, 16 + dy * 4 + dx, device((mx + dx) % 4, (my + dy) % 4, mz, mc)).start()
+    block_copy(me, 32, partner).start()
+
+    def use(k):
+        rows = split3(p_full[k])
+        lanes = pl.ds(pl.multiple_of(k * LANES, LANES), LANES)
+        acc[:, : ev.shape[0]] += fold3(dot_nt(rows, ev[:, lanes]))
+        acc[:, 512:] += fold3(dot_nt(rows, av[:, lanes]))
+
+    order = PLANE_FAR_FIRST[::-1]
+    sources = [((my - dy) % 4) * 4 + (mx - dx) % 4 for dx, dy in order]
+    for n in range(len(order) + LAG):
+        if n < len(order):
+            dx, dy = order[n]
+            block_copy(sources[n], 16 + dy * 4 + dx, partner).wait_recv()
+            block_copy(sources[n], 33 + n, partner).start()
+        if n == 0:
+            block_copy(me, 32, partner).wait_recv()
+            use(me)
+        if n >= LAG:
+            k = n - LAG
+            block_copy(sources[k], 33 + k, partner).wait_recv()
+            use(sources[k])
+    pas = split3(acc[:, 512:])
+    wt = acc[:, : ev.shape[0]] + fold3(dot_nt(pas, gv[...]))
     for g in range(4):
         w_src[g] = wt[8 * g : 8 * g + 8, :]
+    gather_all = remote(x_recv.at[pl.ds(1, 15)], x_recv.at[pl.ds(1, 15)], 3, 3, partner)
+    pair = remote(p_full.at[:, mine, :], p_full.at[:, mine, :], 4, 4, partner)
 
     group = mxh * 2 + mc
 
-    def send_group(j, carry):
+    for j in (2, 3, 1):
         xh, c = group_peer(j)
-        remote(w_src.at[xh * 2 + c], w_recv.at[j], 5, device(xh * 2 + mxl, my, mz, c)).start()
-        return carry
-
-    lax.fori_loop(1, 4, send_group, 0)
-    group_all = remote(w_src.at[pl.ds(1, 3)], w_recv.at[pl.ds(1, 3)], 5, partner)
+        remote(w_src.at[xh * 2 + c], w_recv.at[j], 5, 5, device(xh * 2 + mxl, my, mz, c)).start()
+    group_all = remote(w_src.at[pl.ds(1, 3)], w_recv.at[pl.ds(1, 3)], 5, 5, partner)
 
     p_rows = jnp.concatenate([p_full[b] for b in range(BLOCKS)], axis=1)
     basis_f[...] = p_rows
@@ -230,12 +267,9 @@
     group_all.wait_recv()
     w_z[mz] = w_src[group] + w_recv[1] + w_recv[2] + w_recv[3]
 
-    def send_wz(j, carry):
-        remote(w_z.at[mz], w_z.at[mz], 6, device(mx, my, (mz + j) % 8, mc)).start()
-        return carry
-
-    lax.fori_loop(1, 8, send_wz, 0)
-    wz_all = remote(w_z.at[pl.ds(0, 7)], w_z.at[pl.ds(0, 7)], 6, partner)
+    for dz in Z_ORDER:
+        remote(w_z.at[mz], w_z.at[mz], 6, 6, device(mx, my, (mz + dz) % 8, mc)).start()
+    wz_all = remote(w_z.at[pl.ds(0, 7)], w_z.at[pl.ds(0, 7)], 6, 6, partner)
 
     inverse = inverse_factor(gram)
 
@@ -245,13 +279,10 @@
         total = total + w_z[j]
     w_full[group] = total
 
-    def send_wg(j, carry):
+    for j in (2, 3, 1):
         xh, c = group_peer(j)
-        remote(w_full.at[group], w_full.at[group], 7, device(xh * 2 + mxl, my, mz, c)).start()
-        return carry
-
-    lax.fori_loop(1, 4, send_wg, 0)
-    wg_all = remote(w_recv.at[pl.ds(1, 3)], w_recv.at[pl.ds(1, 3)], 7, partner)
+        remote(w_full.at[group], w_full.at[group], 7, 7, device(xh * 2 + mxl, my, mz, c)).start()
+    wg_all = remote(w_recv.at[pl.ds(1, 3)], w_recv.at[pl.ds(1, 3)], 7, 7, partner)
 
     basis = jnp.dot(inverse, basis_f[...], precision=lax.Precision.HIGHEST, preferred_element_type=F32)
     basis_f[...] = basis
@@ -272,7 +303,8 @@
     q_low = (q - q_high.astype(F32)).astype(BF16)
     q3_ref[...] = jnp.concatenate([q_high, q_high, q_low], axis=1)
 
-    swap.wait_send()
+    for swap in swaps:
+        swap.wait_send()
     plane_all.wait_send()
     z_all.wait_send()
     gather_all.wait_send()
@@ -332,15 +364,15 @@
             pltpu.VMEM((BLOCKS, half, LANES), F32),
             pltpu.VMEM((8, half, LANES), F32),
             pltpu.VMEM((BLOCKS, rank, LANES), F32),
-            pltpu.VMEM((3 * rank, padded), BF16),
+            pltpu.VMEM((rank, 512 + 2 * tokens), F32),
             pltpu.VMEM((4, 8, columns), F32),
             pltpu.VMEM((4, 8, columns), F32),
             pltpu.VMEM((8, 8, columns), F32),
             pltpu.VMEM((4, 8, columns), F32),
             pltpu.VMEM((rank, padded), F32),
             pltpu.SemaphoreType.DMA((16,)),
-            pltpu.SemaphoreType.DMA((8,)),
-            pltpu.SemaphoreType.DMA((8,)),
+            pltpu.SemaphoreType.DMA((12,)),
+            pltpu.SemaphoreType.DMA((48,)),
         ],
         compiler_params=pltpu.CompilerParams(
             collective_id=0, has_side_effects=True, vmem_limit_bytes=28 << 20

time: 51.8 us -> 52.8 us (1.019)
  Pallas kernels: 51 us -> 52.1 us
    pallas_call x1, Pallas kernels: 48.1 us -> 49.2 us  [body(): pl.pallas_call(reduce_kernel, out_shape=(jax.ShapeDtypeStruct((columns, w...]
where the time goes in v2:
time: 52.8 us; the launch traced here: 52.7 us
  Pallas kernels  52.1 us (99%)
  between operations  0.64 us (1%)
    pallas_call x1, Pallas kernels, body(): pl.pallas_call(reduce_kernel, out_shape=(jax.ShapeDtypeStruct((columns, w...  49.2 us
    pallas_call x1, Pallas kernels, body(): pl.pallas_call(error_kernel, out_shape=(jax.ShapeDtypeStruct((columns, wi...  2.9 us

profile of v2, /device:TPU:1, one launch (start us, length us, event | category | flops | bytes accessed | tf_op | source)
XLA Modules:
  0.0 52.7 jit_solution(5759830049771681612)
XLA Ops:
  0.6 49.2 %reduce_kernel.1 = (f32[496,3968]{1,0:T(8,128)S(1)}, bf16[96,3968]{1,0:T(8,128)(2,1)S(1)}, bf16[496,96]{1,0:T(8,128)(2,1)S(1)}, f32[32,496]{1,0:T(8,128)S(1)}, f32[32,124]{1,0:T(8,128)S(1)}) custom-call(f32[32,496]{1,0:T(8,128)} %bitcast.8, bf16[2,496,128]{2,1,0:T(8,128)(2,1)} %bitcast.7, bf16[2,128,3968]{2,1,0:T(8,128)(2,1)} %a_hbm.1, bf16[496,3968]{1,0:T(8,128)(2,1)} %bitcast.6), custom_call_target="tpu_custom_call" | custom-call | tf_op jit(solution)/shard_map/reduce_kernel/pallas_call | solution.py:345
  49.8 2.9 %error_kernel.1 = (bf16[496,3968]{1,0:T(8,128)(2,1)}, f32[32,496]{1,0:T(8,128)}, f32[32,124]{1,0:T(8,128)}) custom-call(f32[496,3968]{1,0:T(8,128)S(1)} %get-tuple-element.11.merged_ref, bf16[96,3968]{1,0:T(8,128)(2,1)S(1)} %get-tuple-element.12.basis3_ref, bf16[496,96]{1,0:T(8,128)(2,1)S(1)} %get-tuple-element.13.q3_ref, ...), custom_call_target="tpu_custom_call" | custom-call | tf_op jit(solution)/shard_map/error_kernel/pallas_call | solution.py:382

commit v3 on v2

--- a/solution.py
+++ b/solution.py
@@ -15,11 +15,15 @@
 ROW_ORDER = (2, 3, 1, 0)
 X_ORDER = (2, 3, 1, 0)
 Z_ORDER = (4, 3, 5, 2, 6, 1, 7)
-PLANE_FAR_FIRST = sorted(
-    ((dx, dy) for dx in range(4) for dy in range(4) if dx + dy),
-    key=lambda d: -(min(d[0], 4 - d[0]) + min(d[1], 4 - d[1])),
+
+
+def hops(step):
+    return sum(min(d, 4 - d) for d in step)
+
+
+SEND_ORDER = sorted(
+    ((dx, dy) for dx in range(4) for dy in range(4) if dx + dy), key=lambda step: (4, 2, 3, 1, 0)[hops(step)]
 )
-LAG = 3
 
 
 def split3(x):
@@ -67,7 +71,7 @@
     q_hbm, g_hbm, a_hbm, e_hbm,
     merged_ref, basis3_ref, q3_ref, qt_ref, pb_ref,
     qv, gv, av, ev,
-    p_part, c_recv, x_src, x_recv, z_buf, p_full, acc,
+    p_part, c_recv, x_src, x_recv, z_buf, p_full, w_acc, a_acc, inv_s,
     w_src, w_recv, w_z, w_full, basis_f,
     load_sem, ssem, rsem,
 ):
@@ -189,13 +193,13 @@
         r = fold3(dot_nn(qs, ev[:, lanes]) + dot_nn(gqs, av[:, lanes]))
         for b in range(4):
             p_part[row * 4 + b] = r[:, b * LANES : (b + 1) * LANES]
-        if i == 0:
-            pl.semaphore_wait(barrier, 24)
+    pl.semaphore_wait(barrier, 24)
+    for i, (dy, row, start, each) in enumerate(pieces):
         four = pl.ds(row * 4, 4)
         swaps.append(remote(p_part.at[four, other, :], c_recv.at[four], 8 + i, 8 + i, partner))
         swaps[i].start()
-        if i > 0:
-            to_plane(i - 1)
+    for i in range(3):
+        to_plane(i)
     to_plane(3)
     plane_all = remote(x_src.at[pl.ds(1, 15)], x_recv.at[pl.ds(1, 15)], 1, 1, partner)
 
@@ -212,7 +216,6 @@
     for dz in Z_ORDER:
         remote(z_buf.at[mz], z_buf.at[mz], 2, 2, device(mx, my, (mz + dz) % 8, mc)).start()
     z_all = remote(z_buf.at[pl.ds(0, 7)], z_buf.at[pl.ds(0, 7)], 2, 2, partner)
-    acc[...] = jnp.zeros_like(acc)
     z_all.wait_recv()
     total = z_buf[0]
     for j in range(1, 8):
@@ -222,32 +225,41 @@
     def block_copy(k, recv, target):
         return remote(p_full.at[k, mine, :], p_full.at[k, mine, :], 3 if recv < 32 else 4, recv, target)
 
-    for dx, dy in PLANE_FAR_FIRST:
+    for dx, dy in SEND_ORDER:
         block_copy(me, 16 + dy * 4 + dx, device((mx + dx) % 4, (my + dy) % 4, mz, mc)).start()
     block_copy(me, 32, partner).start()
 
-    def use(k):
-        rows = split3(p_full[k])
-        lanes = pl.ds(pl.multiple_of(k * LANES, LANES), LANES)
-        acc[:, : ev.shape[0]] += fold3(dot_nt(rows, ev[:, lanes]))
-        acc[:, 512:] += fold3(dot_nt(rows, av[:, lanes]))
-
-    order = PLANE_FAR_FIRST[::-1]
-    sources = [((my - dy) % 4) * 4 + (mx - dx) % 4 for dx, dy in order]
-    for n in range(len(order) + LAG):
-        if n < len(order):
-            dx, dy = order[n]
-            block_copy(sources[n], 16 + dy * 4 + dx, partner).wait_recv()
-            block_copy(sources[n], 33 + n, partner).start()
-        if n == 0:
-            block_copy(me, 32, partner).wait_recv()
-            use(me)
-        if n >= LAG:
-            k = n - LAG
-            block_copy(sources[k], 33 + k, partner).wait_recv()
-            use(sources[k])
-    pas = split3(acc[:, 512:])
-    wt = acc[:, : ev.shape[0]] + fold3(dot_nt(pas, gv[...]))
+    def use(group):
+        w_sum, a_sum = None, None
+        for k, recv in group:
+            block_copy(k, recv, partner).wait_recv()
+        for k, recv in group:
+            rows = split3(p_full[k])
+            lanes = pl.ds(pl.multiple_of(k * LANES, LANES), LANES)
+            w_part = dot_nt(ev[:, lanes], rows)
+            a_part = dot_nt(av[:, lanes], rows)
+            w_sum = w_part if w_sum is None else w_sum + w_part
+            a_sum = a_part if a_sum is None else a_sum + a_part
+        return w_sum, a_sum
+
+    waiting = [(me, 32)]
+    for n, distances in enumerate(((1,), (2,), (3, 4))):
+        arrived = []
+        for dx, dy in SEND_ORDER:
+            if hops((dx, dy)) in distances:
+                k = ((my - dy) % 4) * 4 + (mx - dx) % 4
+                block_copy(k, 16 + dy * 4 + dx, partner).wait_recv()
+                block_copy(k, 32 + dy * 4 + dx, partner).start()
+                arrived.append((k, 32 + dy * 4 + dx))
+        if n > 0:
+            w_sum, a_sum = use(waiting)
+            w_acc[...] = w_sum if n == 1 else w_acc[...] + w_sum
+            a_acc[...] = a_sum if n == 1 else a_acc[...] + a_sum
+            waiting = []
+        waiting = waiting + arrived
+    w_sum, a_sum = use(waiting)
+    pas = split3(fold3((a_acc[...] + a_sum).T))
+    wt = fold3((w_acc[...] + w_sum + dot_nt(gv[...], pas)).T)
     for g in range(4):
         w_src[g] = wt[8 * g : 8 * g + 8, :]
     gather_all = remote(x_recv.at[pl.ds(1, 15)], x_recv.at[pl.ds(1, 15)], 3, 3, partner)
@@ -262,7 +274,7 @@
 
     p_rows = jnp.concatenate([p_full[b] for b in range(BLOCKS)], axis=1)
     basis_f[...] = p_rows
-    gram = dot_nt(p_rows, p_rows, lax.Precision.HIGHEST)
+    inv_s[...] = dot_nt(p_rows, p_rows, lax.Precision.HIGHEST)
 
     group_all.wait_recv()
     w_z[mz] = w_src[group] + w_recv[1] + w_recv[2] + w_recv[3]
@@ -271,7 +283,7 @@
         remote(w_z.at[mz], w_z.at[mz], 6, 6, device(mx, my, (mz + dz) % 8, mc)).start()
     wz_all = remote(w_z.at[pl.ds(0, 7)], w_z.at[pl.ds(0, 7)], 6, 6, partner)
 
-    inverse = inverse_factor(gram)
+    inv_s[...] = inverse_factor(inv_s[...])
 
     wz_all.wait_recv()
     total = w_z[0]
@@ -284,6 +296,7 @@
         remote(w_full.at[group], w_full.at[group], 7, 7, device(xh * 2 + mxl, my, mz, c)).start()
     wg_all = remote(w_recv.at[pl.ds(1, 3)], w_recv.at[pl.ds(1, 3)], 7, 7, partner)
 
+    inverse = inv_s[...]
     basis = jnp.dot(inverse, basis_f[...], precision=lax.Precision.HIGHEST, preferred_element_type=F32)
     basis_f[...] = basis
     high = basis[:, :width].astype(BF16)
@@ -364,7 +377,9 @@
             pltpu.VMEM((BLOCKS, half, LANES), F32),
             pltpu.VMEM((8, half, LANES), F32),
             pltpu.VMEM((BLOCKS, rank, LANES), F32),
-            pltpu.VMEM((rank, 512 + 2 * tokens), F32),
+            pltpu.VMEM((columns, 3 * rank), F32),
+            pltpu.VMEM((2 * tokens, 3 * rank), F32),
+            pltpu.VMEM((rank, rank), F32),
             pltpu.VMEM((4, 8, columns), F32),
             pltpu.VMEM((4, 8, columns), F32),
             pltpu.VMEM((8, 8, columns), F32),

time: 52.8 us -> 48.9 us (0.926)
  Pallas kernels: 52.1 us -> 48.2 us
    pallas_call x1, Pallas kernels: 49.2 us -> 45.3 us  [body(): pl.pallas_call(reduce_kernel, out_shape=(jax.ShapeDtypeStruct((columns, w...]
where the time goes in v3:
time: 48.9 us; the launch traced here: 48.8 us
  Pallas kernels  48.2 us (99%)
  between operations  0.64 us (1%)
    pallas_call x1, Pallas kernels, body(): pl.pallas_call(reduce_kernel, out_shape=(jax.ShapeDtypeStruct((columns, w...  45.3 us
    pallas_call x1, Pallas kernels, body(): pl.pallas_call(error_kernel, out_shape=(jax.ShapeDtypeStruct((columns, wi...  2.9 us

profile of v3, /device:TPU:1, one launch (start us, length us, event | category | flops | bytes accessed | tf_op | source)
XLA Modules:
  0.0 48.8 jit_solution(7950538575695573757)
XLA Ops:
  0.6 45.3 %reduce_kernel.1 = (f32[496,3968]{1,0:T(8,128)S(1)}, bf16[96,3968]{1,0:T(8,128)(2,1)S(1)}, bf16[496,96]{1,0:T(8,128)(2,1)S(1)}, f32[32,496]{1,0:T(8,128)S(1)}, f32[32,124]{1,0:T(8,128)S(1)}) custom-call(f32[32,496]{1,0:T(8,128)} %bitcast.8, bf16[2,496,128]{2,1,0:T(8,128)(2,1)} %bitcast.7, bf16[2,128,3968]{2,1,0:T(8,128)(2,1)} %a_hbm.1, bf16[496,3968]{1,0:T(8,128)(2,1)} %bitcast.6), custom_call_target="tpu_custom_call" | custom-call | tf_op jit(solution)/shard_map/reduce_kernel/pallas_call | solution.py:358
  45.9 2.9 %error_kernel.1 = (bf16[496,3968]{1,0:T(8,128)(2,1)}, f32[32,496]{1,0:T(8,128)}, f32[32,124]{1,0:T(8,128)}) custom-call(f32[496,3968]{1,0:T(8,128)S(1)} %get-tuple-element.11.merged_ref, bf16[96,3968]{1,0:T(8,128)(2,1)S(1)} %get-tuple-element.12.basis3_ref, bf16[496,96]{1,0:T(8,128)(2,1)S(1)} %get-tuple-element.13.q3_ref, ...), custom_call_target="tpu_custom_call" | custom-call | tf_op jit(solution)/shard_map/error_kernel/pallas_call | solution.py:397

commit v4 on v3

--- a/solution.py
+++ b/solution.py
@@ -14,7 +14,10 @@
 LANES = 256
 ROW_ORDER = (2, 3, 1, 0)
 X_ORDER = (2, 3, 1, 0)
-Z_ORDER = (4, 3, 5, 2, 6, 1, 7)
+BARRIER_AT = 2
+P_PARTS = 2
+P_Z_ORDER = (4, 3, 5, 2, 6, 1, 7, 0)
+W_Z_ORDER = (0, 1, 2, 3, 4, 5, 6, 7)
 
 
 def hops(step):
@@ -26,12 +29,25 @@
 )
 
 
-def split3(x):
+def split_parts(x):
     high = x.astype(BF16)
     rest = x - high.astype(F32)
     middle = rest.astype(BF16)
-    low = (rest - middle.astype(F32)).astype(BF16)
-    return jnp.concatenate([high, middle, low], axis=0)
+    return high, middle, (rest - middle.astype(F32)).astype(BF16)
+
+
+def split3(x):
+    return jnp.concatenate(split_parts(x), axis=0)
+
+
+def factor_terms(x):
+    high, middle, low = split_parts(x)
+    return jnp.concatenate([high, middle, low, high, middle, high], axis=1)
+
+
+def rows_terms(y):
+    high, middle, low = split_parts(y)
+    return jnp.concatenate([high, high, high, middle, middle, low], axis=0)
 
 
 def fold3(x):
@@ -173,19 +189,27 @@
             device_id=target, device_id_type=MESH,
         )
 
+    def along_z(order, send):
+        for z in order:
+
+            @pl.when(z != mz)
+            def _(z=z):
+                send(device(mx, my, z, mc))
+
     mine = pl.ds(pl.multiple_of(mc * half, half), half)
     other = pl.ds(pl.multiple_of(((mc + 1) % 2) * half, half), half)
     swaps = []
 
-    def to_plane(i):
+    cuts = [pl.ds(h * (half // P_PARTS), half // P_PARTS) for h in range(P_PARTS)]
+
+    def to_plane(i, h):
         dy, row, _, _ = pieces[i]
-        four = pl.ds(row * 4, 4)
-        swaps[i].wait_recv()
-        x_src[four] = p_part[four, mine, :] + c_recv[four]
         for dx in X_ORDER:
             if dx + dy > 0:
                 x = (mx + dx) % 4
-                remote(x_src.at[row * 4 + x], x_recv.at[dy * 4 + dx], 1, 1, device(x, row, mz, mc)).start()
+                remote(
+                    x_src.at[row * 4 + x, cuts[h], :], x_recv.at[dy * 4 + dx, cuts[h], :], 1, 12 + h, device(x, row, mz, mc)
+                ).start()
 
     for i, (dy, row, start, each) in enumerate(pieces):
         each(lambda cp: cp.wait())
@@ -193,40 +217,55 @@
         r = fold3(dot_nn(qs, ev[:, lanes]) + dot_nn(gqs, av[:, lanes]))
         for b in range(4):
             p_part[row * 4 + b] = r[:, b * LANES : (b + 1) * LANES]
-    pl.semaphore_wait(barrier, 24)
+        four = pl.ds(row * 4, 4)
+        swaps.append(remote(p_part.at[four, other, :], c_recv.at[four], 8 + i, 8 + i, partner))
+        if i == BARRIER_AT:
+            pl.semaphore_wait(barrier, 24)
+            for swap in swaps[:i]:
+                swap.start()
+        if i >= BARRIER_AT:
+            swaps[i].start()
     for i, (dy, row, start, each) in enumerate(pieces):
         four = pl.ds(row * 4, 4)
-        swaps.append(remote(p_part.at[four, other, :], c_recv.at[four], 8 + i, 8 + i, partner))
-        swaps[i].start()
-    for i in range(3):
-        to_plane(i)
-    to_plane(3)
+        swaps[i].wait_recv()
+        x_src[four] = p_part[four, mine, :] + c_recv[four]
+        to_plane(i, 0)
+    for h in range(1, P_PARTS):
+        for i in range(4):
+            to_plane(i, h)
     plane_all = remote(x_src.at[pl.ds(1, 15)], x_recv.at[pl.ds(1, 15)], 1, 1, partner)
 
     for s in range(0, width, 512):
         n = min(512, width - s)
         merged_ref[:, s : s + n] = dot_nn(gv[...], av[:, s : s + n]) + ev[:, s : s + n].astype(F32)
 
-    plane_all.wait_recv()
-    total = x_src[me]
-    for j in range(1, 16):
-        total = total + x_recv[j]
-    z_buf[mz] = total
-
-    for dz in Z_ORDER:
-        remote(z_buf.at[mz], z_buf.at[mz], 2, 2, device(mx, my, (mz + dz) % 8, mc)).start()
+    for h, cut in enumerate(cuts):
+        arrivals = x_recv.at[pl.ds(1, 15), cut, :]
+        remote(arrivals, arrivals, 1, 12 + h, partner).wait_recv()
+        total = x_src[me, cut, :]
+        for j in range(1, 16):
+            total = total + x_recv[j, cut, :]
+        z_buf[mz, cut, :] = total
+        block = z_buf.at[mz, cut, :]
+        along_z(P_Z_ORDER, lambda target, block=block, h=h: remote(block, block, 2, 14 + h, target).start())
     z_all = remote(z_buf.at[pl.ds(0, 7)], z_buf.at[pl.ds(0, 7)], 2, 2, partner)
-    z_all.wait_recv()
-    total = z_buf[0]
-    for j in range(1, 8):
-        total = total + z_buf[j]
-    p_full[me, mine, :] = total
+    for h, cut in enumerate(cuts):
+        arrivals = z_buf.at[pl.ds(0, 7), cut, :]
+        remote(arrivals, arrivals, 2, 14 + h, partner).wait_recv()
+        total = z_buf[0, cut, :]
+        for j in range(1, 8):
+            total = total + z_buf[j, cut, :]
+        rows = pl.ds(pl.multiple_of(mc * half + h * (half // P_PARTS), 8), half // P_PARTS)
+        p_full[me, rows, :] = total
+        block = p_full.at[me, rows, :]
+        for dx, dy in SEND_ORDER:
+            remote(
+                block, block, 3, 16 + dy * 4 + dx, device((mx + dx) % 4, (my + dy) % 4, mz, mc)
+            ).start()
 
     def block_copy(k, recv, target):
         return remote(p_full.at[k, mine, :], p_full.at[k, mine, :], 3 if recv < 32 else 4, recv, target)
 
-    for dx, dy in SEND_ORDER:
-        block_copy(me, 16 + dy * 4 + dx, device((mx + dx) % 4, (my + dy) % 4, mz, mc)).start()
     block_copy(me, 32, partner).start()
 
     def use(group):
@@ -237,7 +276,7 @@
             rows = split3(p_full[k])
             lanes = pl.ds(pl.multiple_of(k * LANES, LANES), LANES)
             w_part = dot_nt(ev[:, lanes], rows)
-            a_part = dot_nt(av[:, lanes], rows)
+            a_part = dot_nt(rows, av[:, lanes])
             w_sum = w_part if w_sum is None else w_sum + w_part
             a_sum = a_part if a_sum is None else a_sum + a_part
         return w_sum, a_sum
@@ -258,7 +297,7 @@
             waiting = []
         waiting = waiting + arrived
     w_sum, a_sum = use(waiting)
-    pas = split3(fold3((a_acc[...] + a_sum).T))
+    pas = split3(fold3(a_acc[...] + a_sum))
     wt = fold3((w_acc[...] + w_sum + dot_nt(gv[...], pas)).T)
     for g in range(4):
         w_src[g] = wt[8 * g : 8 * g + 8, :]
@@ -267,36 +306,45 @@
 
     group = mxh * 2 + mc
 
-    for j in (2, 3, 1):
-        xh, c = group_peer(j)
-        remote(w_src.at[xh * 2 + c], w_recv.at[j], 5, 5, device(xh * 2 + mxl, my, mz, c)).start()
+    columns = w_src.shape[2]
+    strips = [pl.ds(0, columns)]
+    for h, strip in enumerate(strips):
+        for j in (2, 3, 1):
+            xh, c = group_peer(j)
+            remote(
+                w_src.at[xh * 2 + c, :, strip], w_recv.at[j, :, strip], 5, 5 + 2 * h, device(xh * 2 + mxl, my, mz, c)
+            ).start()
     group_all = remote(w_src.at[pl.ds(1, 3)], w_recv.at[pl.ds(1, 3)], 5, 5, partner)
 
     p_rows = jnp.concatenate([p_full[b] for b in range(BLOCKS)], axis=1)
     basis_f[...] = p_rows
     inv_s[...] = dot_nt(p_rows, p_rows, lax.Precision.HIGHEST)
 
-    group_all.wait_recv()
-    w_z[mz] = w_src[group] + w_recv[1] + w_recv[2] + w_recv[3]
-
-    for dz in Z_ORDER:
-        remote(w_z.at[mz], w_z.at[mz], 6, 6, device(mx, my, (mz + dz) % 8, mc)).start()
+    for h, strip in enumerate(strips):
+        arrivals = w_recv.at[pl.ds(1, 3), :, strip]
+        remote(arrivals, arrivals, 5, 5 + 2 * h, partner).wait_recv()
+        w_z[mz, :, strip] = w_src[group, :, strip] + w_recv[1, :, strip] + w_recv[2, :, strip] + w_recv[3, :, strip]
+        block = w_z.at[mz, :, strip]
+        along_z(W_Z_ORDER, lambda target, block=block, h=h: remote(block, block, 6, h, target).start())
     wz_all = remote(w_z.at[pl.ds(0, 7)], w_z.at[pl.ds(0, 7)], 6, 6, partner)
 
     inv_s[...] = inverse_factor(inv_s[...])
 
-    wz_all.wait_recv()
-    total = w_z[0]
-    for j in range(1, 8):
-        total = total + w_z[j]
-    w_full[group] = total
-
-    for j in (2, 3, 1):
-        xh, c = group_peer(j)
-        remote(w_full.at[group], w_full.at[group], 7, 7, device(xh * 2 + mxl, my, mz, c)).start()
-    wg_all = remote(w_recv.at[pl.ds(1, 3)], w_recv.at[pl.ds(1, 3)], 7, 7, partner)
+    for h, strip in enumerate(strips):
+        arrivals = w_z.at[pl.ds(0, 7), :, strip]
+        remote(arrivals, arrivals, 6, h, partner).wait_recv()
+        total = w_z[0, :, strip]
+        for j in range(1, 8):
+            total = total + w_z[j, :, strip]
+        w_full[group, :, strip] = total
+        block = w_full.at[group, :, strip]
+        for j in (2, 3, 1):
+            xh, c = group_peer(j)
+            remote(block, block, 7, 6, device(xh * 2 + mxl, my, mz, c)).start()
+    wg_all = remote(w_recv.at[pl.ds(1, 3)], w_recv.at[pl.ds(1, 3)], 7, 6, partner)
 
     inverse = inv_s[...]
+    inverse_terms = factor_terms(inverse * (1.0 / 32))
     basis = jnp.dot(inverse, basis_f[...], precision=lax.Precision.HIGHEST, preferred_element_type=F32)
     basis_f[...] = basis
     high = basis[:, :width].astype(BF16)
@@ -309,12 +357,10 @@
 
     wg_all.wait_recv()
     w_rows = jnp.concatenate([w_full[g] for g in range(4)], axis=0)
-    qt = jnp.dot(inverse, w_rows, precision=lax.Precision.HIGHEST, preferred_element_type=F32) * (1.0 / 32)
+    qt = dot_nn(inverse_terms, rows_terms(w_rows))
     qt_ref[...] = qt
-    q = qt.T
-    q_high = q.astype(BF16)
-    q_low = (q - q_high.astype(F32)).astype(BF16)
-    q3_ref[...] = jnp.concatenate([q_high, q_high, q_low], axis=1)
+    q_high = qt.astype(BF16).astype(F32)
+    q3_ref[...] = jnp.concatenate([q_high, q_high, qt - q_high], axis=0).T.astype(BF16)
 
     for swap in swaps:
         swap.wait_send()
@@ -378,7 +424,7 @@
             pltpu.VMEM((8, half, LANES), F32),
             pltpu.VMEM((BLOCKS, rank, LANES), F32),
             pltpu.VMEM((columns, 3 * rank), F32),
-            pltpu.VMEM((2 * tokens, 3 * rank), F32),
+            pltpu.VMEM((3 * rank, 2 * tokens), F32),
             pltpu.VMEM((rank, rank), F32),
             pltpu.VMEM((4, 8, columns), F32),
             pltpu.VMEM((4, 8, columns), F32),

time: 48.9 us -> 47.8 us (0.978)
  Pallas kernels: 48.2 us -> 47 us
    pallas_call x1, Pallas kernels: 45.3 us -> 44.1 us  [body(): pl.pallas_call(reduce_kernel, out_shape=(jax.ShapeDtypeStruct((columns, w...]
where the time goes in v4:
time: 47.8 us; the launch traced here: 47.7 us
  Pallas kernels  47 us (98%)
  between operations  0.64 us (1%)
    pallas_call x1, Pallas kernels, body(): pl.pallas_call(reduce_kernel, out_shape=(jax.ShapeDtypeStruct((columns, w...  44.1 us
    pallas_call x1, Pallas kernels, body(): pl.pallas_call(error_kernel, out_shape=(jax.ShapeDtypeStruct((columns, wi...  2.9 us

profile of v4, /device:TPU:1, one launch (start us, length us, event | category | flops | bytes accessed | tf_op | source)
XLA Modules:
  0.0 47.7 jit_solution(5185091233053266328)
XLA Ops:
  0.6 44.1 %reduce_kernel.1 = (f32[496,3968]{1,0:T(8,128)S(1)}, bf16[96,3968]{1,0:T(8,128)(2,1)S(1)}, bf16[496,96]{1,0:T(8,128)(2,1)S(1)}, f32[32,496]{1,0:T(8,128)S(1)}, f32[32,124]{1,0:T(8,128)S(1)}) custom-call(f32[32,496]{1,0:T(8,128)} %bitcast.8, bf16[2,496,128]{2,1,0:T(8,128)(2,1)} %bitcast.7, bf16[2,128,3968]{2,1,0:T(8,128)(2,1)} %a_hbm.1, bf16[496,3968]{1,0:T(8,128)(2,1)} %bitcast.6), custom_call_target="tpu_custom_call" | custom-call | tf_op jit(solution)/shard_map/reduce_kernel/pallas_call | solution.py:404
  44.8 2.9 %error_kernel.1 = (bf16[496,3968]{1,0:T(8,128)(2,1)}, f32[32,496]{1,0:T(8,128)}, f32[32,124]{1,0:T(8,128)}) custom-call(f32[496,3968]{1,0:T(8,128)S(1)} %get-tuple-element.11.merged_ref, bf16[96,3968]{1,0:T(8,128)(2,1)S(1)} %get-tuple-element.12.basis3_ref, bf16[496,96]{1,0:T(8,128)(2,1)S(1)} %get-tuple-element.13.q3_ref, ...), custom_call_target="tpu_custom_call" | custom-call | tf_op jit(solution)/shard_map/error_kernel/pallas_call | solution.py:443

commit v5 on v4

--- a/solution.py
+++ b/solution.py
@@ -96,21 +96,24 @@
     width = e_hbm.shape[1]
     share = pb_ref.shape[1]
     dp, mp = lax.axis_index("dp"), lax.axis_index("mp")
-    mz, mxh, mc = dp // 4, (dp // 2) % 2, dp % 2
-    my, mxl = mp // 2, mp % 2
+    mz, mxh, mc = lax.div(dp, 4), lax.rem(lax.div(dp, 2), 2), lax.rem(dp, 2)
+    my, mxl = lax.div(mp, 2), lax.rem(mp, 2)
     mx = mxh * 2 + mxl
     me = my * 4 + mx
-
-    def device(x, y, z, c):
-        return ((z * 2 + x // 2) * 2 + c, y * 2 + x % 2)
-
-    def plane_peer(j):
-        return (mx + j % 4) % 4, (my + j // 4) % 4
-
-    def group_peer(j):
-        return (mxh + j // 2) % 2, (mc + j % 2) % 2
-
-    partner = device(mx, my, mz, (mc + 1) % 2)
+    oc = 1 - mc
+
+    xs = [lax.rem(mx + d, 4) for d in range(4)]
+    ys = [lax.rem(my + d, 4) for d in range(4)]
+    x_dp = [(mz * 2 + lax.div(x, 2)) * 2 + mc for x in xs]
+    x_mp = [lax.rem(x, 2) for x in xs]
+    plane = {(dx, dy): (x_dp[dx], ys[dy] * 2 + x_mp[dx]) for dx in range(4) for dy in range(4)}
+    line = [((z * 2 + mxh) * 2 + mc, mp) for z in range(8)]
+    partner = (dp + 1 - 2 * mc, mp)
+    group = mxh * 2 + mc
+    group_peers = {}
+    for j in (1, 2, 3):
+        xh, c = (1 - mxh if j >= 2 else mxh), (oc if j % 2 else mc)
+        group_peers[j] = (xh * 2 + c, ((mz * 2 + xh) * 2 + c, mp))
 
     tokens = a_hbm.shape[1]
     padded = ev.shape[1]
@@ -125,7 +128,7 @@
     short = width - 3 * step
     pieces = []
     for i, dy in enumerate(ROW_ORDER):
-        row = (my + dy) % 4
+        row = ys[dy]
         start = pl.multiple_of(row * step, step)
 
         def piece_copies(n, start=start, i=i):
@@ -158,21 +161,16 @@
     def greet(target):
         pl.semaphore_signal(barrier, inc=1, device_id=target, device_id_type=MESH)
 
+    for step_xy in SEND_ORDER:
+        greet(plane[step_xy])
+    for z in range(8):
+
+        @pl.when(z != mz)
+        def _(z=z):
+            greet(line[z])
+
     greet(partner)
-
-    def greet_plane(j, carry):
-        x, y = plane_peer(j)
-        greet(device(x, y, mz, mc))
-        return carry
-
-    lax.fori_loop(1, 16, greet_plane, 0)
-
-    def greet_z(j, carry):
-        greet(device(mx, my, (mz + j) % 8, mc))
-        return carry
-
-    lax.fori_loop(1, 8, greet_z, 0)
-    greet(device(((mxh + 1) % 2) * 2 + mxl, my, mz, (mc + 1) % 2))
+    greet(group_peers[3][1])
 
     ev[:, width:] = jnp.zeros((ev.shape[0], padded - width), BF16)
     av[:, width:] = jnp.zeros((av.shape[0], padded - width), BF16)
@@ -194,10 +192,10 @@
 
             @pl.when(z != mz)
             def _(z=z):
-                send(device(mx, my, z, mc))
+                send(line[z])
 
     mine = pl.ds(pl.multiple_of(mc * half, half), half)
-    other = pl.ds(pl.multiple_of(((mc + 1) % 2) * half, half), half)
+    other = pl.ds(pl.multiple_of(oc * half, half), half)
     swaps = []
 
     cuts = [pl.ds(h * (half // P_PARTS), half // P_PARTS) for h in range(P_PARTS)]
@@ -206,9 +204,8 @@
         dy, row, _, _ = pieces[i]
         for dx in X_ORDER:
             if dx + dy > 0:
-                x = (mx + dx) % 4
                 remote(
-                    x_src.at[row * 4 + x, cuts[h], :], x_recv.at[dy * 4 + dx, cuts[h], :], 1, 12 + h, device(x, row, mz, mc)
+                    x_src.at[row * 4 + xs[dx], cuts[h], :], x_recv.at[dy * 4 + dx, cuts[h], :], 1, 12 + h, plane[dx, dy]
                 ).start()
 
     for i, (dy, row, start, each) in enumerate(pieces):
@@ -259,20 +256,18 @@
         p_full[me, rows, :] = total
         block = p_full.at[me, rows, :]
         for dx, dy in SEND_ORDER:
-            remote(
-                block, block, 3, 16 + dy * 4 + dx, device((mx + dx) % 4, (my + dy) % 4, mz, mc)
-            ).start()
+            remote(block, block, 3, 16 + dy * 4 + dx, plane[dx, dy]).start()
 
     def block_copy(k, recv, target):
         return remote(p_full.at[k, mine, :], p_full.at[k, mine, :], 3 if recv < 32 else 4, recv, target)
 
     block_copy(me, 32, partner).start()
 
-    def use(group):
+    def use(blocks):
         w_sum, a_sum = None, None
-        for k, recv in group:
+        for k, recv in blocks:
             block_copy(k, recv, partner).wait_recv()
-        for k, recv in group:
+        for k, recv in blocks:
             rows = split3(p_full[k])
             lanes = pl.ds(pl.multiple_of(k * LANES, LANES), LANES)
             w_part = dot_nt(ev[:, lanes], rows)
@@ -286,7 +281,7 @@
         arrived = []
         for dx, dy in SEND_ORDER:
             if hops((dx, dy)) in distances:
-                k = ((my - dy) % 4) * 4 + (mx - dx) % 4
+                k = ys[-dy % 4] * 4 + xs[-dx % 4]
                 block_copy(k, 16 + dy * 4 + dx, partner).wait_recv()
                 block_copy(k, 32 + dy * 4 + dx, partner).start()
                 arrived.append((k, 32 + dy * 4 + dx))
@@ -304,16 +299,12 @@
     gather_all = remote(x_recv.at[pl.ds(1, 15)], x_recv.at[pl.ds(1, 15)], 3, 3, partner)
     pair = remote(p_full.at[:, mine, :], p_full.at[:, mine, :], 4, 4, partner)
 
-    group = mxh * 2 + mc
-
     columns = w_src.shape[2]
     strips = [pl.ds(0, columns)]
     for h, strip in enumerate(strips):
         for j in (2, 3, 1):
-            xh, c = group_peer(j)
-            remote(
-                w_src.at[xh * 2 + c, :, strip], w_recv.at[j, :, strip], 5, 5 + 2 * h, device(xh * 2 + mxl, my, mz, c)
-            ).start()
+            place, target = group_peers[j]
+            remote(w_src.at[place, :, strip], w_recv.at[j, :, strip], 5, 5 + 2 * h, target).start()
     group_all = remote(w_src.at[pl.ds(1, 3)], w_recv.at[pl.ds(1, 3)], 5, 5, partner)
 
     p_rows = jnp.concatenate([p_full[b] for b in range(BLOCKS)], axis=1)
@@ -339,8 +330,7 @@
         w_full[group, :, strip] = total
         block = w_full.at[group, :, strip]
         for j in (2, 3, 1):
-            xh, c = group_peer(j)
-            remote(block, block, 7, 6, device(xh * 2 + mxl, my, mz, c)).start()
+            remote(block, block, 7, 6, group_peers[j][1]).start()
     wg_all = remote(w_recv.at[pl.ds(1, 3)], w_recv.at[pl.ds(1, 3)], 7, 6, partner)
 
     inverse = inv_s[...]
@@ -351,9 +341,9 @@
     low = (basis[:, :width] - high.astype(F32)).astype(BF16)
     basis3_ref[...] = jnp.concatenate([high, low, high], axis=0)
     start = dp * share
-    base = pl.multiple_of((start // 128) * 128, 128)
+    base = pl.multiple_of(lax.div(start, 128) * 128, 128)
     window = basis_f[:, pl.ds(base, 256)]
-    pb_ref[...] = pltpu.roll(window, (256 - start % 128) % 256, 1)[:, :share]
+    pb_ref[...] = pltpu.roll(window, lax.rem(256 - lax.rem(start, 128), 256), 1)[:, :share]
 
     wg_all.wait_recv()
     w_rows = jnp.concatenate([w_full[g] for g in range(4)], axis=0)

time: 47.8 us -> 47.5 us (level)
  no operation moved by 1% of the time
where the time goes in v5:
time: 47.5 us; the launch traced here: 47.4 us
  Pallas kernels  46.8 us (99%)
  between operations  0.64 us (1%)
    pallas_call x1, Pallas kernels, body(): pl.pallas_call(reduce_kernel, out_shape=(jax.ShapeDtypeStruct((columns, w...  43.9 us
    pallas_call x1, Pallas kernels, body(): pl.pallas_call(error_kernel, out_shape=(jax.ShapeDtypeStruct((columns, wi...  2.9 us

profile of v5, /device:TPU:1, one launch (start us, length us, event | category | flops | bytes accessed | tf_op | source)
XLA Modules:
  0.0 47.4 jit_solution(12152162224589538563)
XLA Ops:
  0.6 43.9 %reduce_kernel.1 = (f32[496,3968]{1,0:T(8,128)S(1)}, bf16[96,3968]{1,0:T(8,128)(2,1)S(1)}, bf16[496,96]{1,0:T(8,128)(2,1)S(1)}, f32[32,496]{1,0:T(8,128)S(1)}, f32[32,124]{1,0:T(8,128)S(1)}) custom-call(f32[32,496]{1,0:T(8,128)} %bitcast.8, bf16[2,496,128]{2,1,0:T(8,128)(2,1)} %bitcast.7, bf16[2,128,3968]{2,1,0:T(8,128)(2,1)} %a_hbm.1, bf16[496,3968]{1,0:T(8,128)(2,1)} %bitcast.6), custom_call_target="tpu_custom_call" | custom-call | tf_op jit(solution)/shard_map/reduce_kernel/pallas_call | solution.py:394
  44.5 2.9 %error_kernel.1 = (bf16[496,3968]{1,0:T(8,128)(2,1)}, f32[32,496]{1,0:T(8,128)}, f32[32,124]{1,0:T(8,128)}) custom-call(f32[496,3968]{1,0:T(8,128)S(1)} %get-tuple-element.11.merged_ref, bf16[96,3968]{1,0:T(8,128)(2,1)S(1)} %get-tuple-element.12.basis3_ref, bf16[496,96]{1,0:T(8,128)(2,1)S(1)} %get-tuple-element.13.q3_ref, ...), custom_call_target="tpu_custom_call" | custom-call | tf_op jit(solution)/shard_map/error_kernel/pallas_call | solution.py:433
